TPU v7x, 32 devices: a whole 2x2x4 slice. The times are simulated.
32 devices in a mesh: dp: 4 (over z), seq: 4 (over y, core), tensor: 2 (over x).
Axes of the slice: x: 2, y: 2, z: 4, core: 2. Of those that a mesh axis runs over, the one named last changes fastest.
Arguments:
- q_self: bfloat16 [4, 512, 4096], P('dp', 'seq', 'tensor'), may hold values from -162 to 162
- k_self: bfloat16 [4, 512, 1024], P('dp', 'seq', 'tensor'), may hold values from -6 to 6
- v_self: bfloat16 [4, 512, 1024], P('dp', 'seq', 'tensor'), may hold values from -6 to 6
- docs: int32 [4, 512], P('dp', 'seq'), may hold values from 0 to 3, never falling along the last dimension, each value on 1 to 384 neighbouring positions
- q_cross: bfloat16 [4, 512, 4096], P('dp', 'seq', 'tensor'), may hold values from -162 to 162
- cotangent: bfloat16 [4, 512, 4096], P('dp', 'seq', 'tensor'), may hold values from -6 to 6
- img_keys: bfloat16 [4, 128, 1024], P('dp', 'seq', 'tensor'), may hold values from -6 to 6
- features: bfloat16 [4, 128, 1280], P('dp', 'seq'), may hold values from -6 to 6
- w_value: bfloat16 [1280, 1024], P(None, 'tensor'), may hold values from -0.15625 to 0.15625
- tiles: int32 [4, 4], P('dp'), may hold values from 1 to 4
- cite: int32 [4, 4], P('dp'), may hold values from 0 to 3, each once within a row
Outputs:
- combined: bfloat16 [4, 512, 4096], P('dp', 'seq', 'tensor')
- weight_grad: float32 [1280, 1024], P(('dp', 'seq'), 'tensor')
Inputs may be any that keep to these rules, and one draw needn't show every extreme that they name: `docs`: along each sample the document numbers never fall; every document 0 to 3 has one or more tokens. `cite`: each sample's row names every image exactly once.
All inputs are finite; a program needn't handle non-finite values.
Results may differ from a plain program's by a relative error of at most 0.029.
Values may be sent and summed in bfloat16 or wider, within the bound.
No kernel may reach another device: no remote copies, remote signals or barrier semaphores. Data moves between devices by JAX's collectives and lax.ppermute only.
A program may use at most 64 MiB of HBM per device.

v0:
```python
import math
import jax
import jax.numpy as jnp
from jax import lax
from jax.sharding import PartitionSpec as P

HD = 128
TILE_TOK = 8
MASK_FILL = -1e30


def absorb_block(
    running, queries, key_rows, value_rows, key_docs, key_pos, query_pos, my_docs, score_scale
):
    running_max, denominator, numerator = running
    kv_local = queries.shape[1]
    key_count = key_rows.shape[0]
    key_heads = key_rows.reshape(key_count, kv_local, HD)
    value_heads = value_rows.reshape(key_count, kv_local, HD)
    scores = (
        jnp.einsum("tgcd,sgd->gcts", queries, key_heads, preferred_element_type=jnp.float32)
        * score_scale
    )
    kept = (query_pos[:, None] >= key_pos[None, :]) & (my_docs[:, None] == key_docs[None, :])
    scores = jnp.where(kept, scores, MASK_FILL)
    new_max = jnp.maximum(running_max, jnp.max(scores, axis=-1))
    factor = jnp.exp(running_max - new_max)
    weights = jnp.where(kept, jnp.exp(scores - new_max[..., None]), 0.0)
    denominator = factor * denominator + jnp.sum(weights, axis=-1)
    numerator = factor[..., None] * numerator + jnp.einsum(
        "gcts,sgd->gctd",
        weights.astype(jnp.bfloat16),
        value_heads,
        preferred_element_type=jnp.float32,
    )
    return (new_max, denominator, numerator)


def on_device(
    q_self, k_self, v_self, docs, q_cross, cotangent, img_keys, features, w_value, tiles, cite
):
    tok_rows = q_self.shape[1]
    kv_local = k_self.shape[2] // HD
    heads_local = q_self.shape[2] // HD
    group_size = heads_local // kv_local
    score_scale = HD ** (-0.5)
    first_row = lax.axis_index("seq") * tok_rows
    query_pos = first_row + jnp.arange(tok_rows, dtype=jnp.int32)
    my_docs = docs[0]
    queries = q_self[0].reshape(tok_rows, kv_local, group_size, HD)
    start_state = (
        jnp.full((kv_local, group_size, tok_rows), MASK_FILL, jnp.float32),
        jnp.zeros((kv_local, group_size, tok_rows), jnp.float32),
        jnp.zeros((kv_local, group_size, tok_rows, HD), jnp.float32),
    )
    piece_keys = lax.all_gather(k_self, "seq", axis=1, tiled=True)
    piece_values = lax.all_gather(v_self, "seq", axis=1, tiled=True)
    piece_docs = lax.all_gather(docs, "seq", axis=1, tiled=True)
    key_count = piece_keys.shape[1]
    block_rows = math.gcd(key_count, 512)
    block_count = key_count // block_rows
    key_blocks = piece_keys[0].reshape(block_count, block_rows, -1)
    value_blocks = piece_values[0].reshape(block_count, block_rows, -1)
    doc_blocks = piece_docs[0].reshape(block_count, block_rows)
    pos_blocks = jnp.arange(key_count, dtype=jnp.int32).reshape(block_count, block_rows)

    def absorb_step(state_now, block_item):
        key_part, value_part, doc_part, pos_part = block_item
        return (
            absorb_block(
                state_now,
                queries,
                key_part,
                value_part,
                doc_part,
                pos_part,
                query_pos,
                my_docs,
                score_scale,
            ),
            None,
        )

    running_max, denominator, numerator = lax.scan(
        absorb_step, start_state, (key_blocks, value_blocks, doc_blocks, pos_blocks)
    )[0]
    self_out = numerator / denominator[..., None]
    values_own = jnp.dot(features[0], w_value, preferred_element_type=jnp.float32).astype(
        jnp.bfloat16
    )
    image_keys, image_values = (
        lax.all_gather(img_keys[0], "seq", axis=0, tiled=True),
        lax.all_gather(values_own, "seq", axis=0, tiled=True),
    )
    key_count = image_keys.shape[0]
    slot_count = img_keys.shape[1]
    image_count = tiles.shape[1]
    doc_hit = my_docs[:, None] == jnp.arange(cite.shape[1], dtype=jnp.int32)[None, :]
    image_of = jnp.sum(jnp.where(doc_hit, cite[0][None, :], 0), axis=1)
    slot_ids = jnp.arange(key_count, dtype=jnp.int32)
    key_image = slot_ids // slot_count
    owner_hit = key_image[:, None] == jnp.arange(image_count, dtype=jnp.int32)[None, :]
    tile_limit = jnp.sum(jnp.where(owner_hit, tiles[0][None, :], 0), axis=1) * TILE_TOK
    cross_kept = (image_of[:, None] == key_image[None, :]) & (slot_ids % slot_count < tile_limit)[
        None, :
    ]
    cross_q = q_cross[0].reshape(tok_rows, kv_local, group_size, HD)
    cross_scores = (
        jnp.einsum(
            "tgcd,sgd->gcts",
            cross_q,
            image_keys.reshape(key_count, kv_local, HD),
            preferred_element_type=jnp.float32,
        )
        * score_scale
    )
    cross_scores = jnp.where(cross_kept, cross_scores, MASK_FILL)
    cross_exp = jnp.where(
        cross_kept, jnp.exp(cross_scores - jnp.max(cross_scores, axis=-1, keepdims=True)), 0.0
    )
    cross_weights = (cross_exp / jnp.sum(cross_exp, axis=-1, keepdims=True)).astype(jnp.bfloat16)
    cross_out = jnp.einsum(
        "gcts,sgd->gctd",
        cross_weights,
        image_values.reshape(key_count, kv_local, HD),
        preferred_element_type=jnp.float32,
    )
    merged = (
        (self_out + cross_out)
        .astype(jnp.bfloat16)
        .transpose(2, 0, 1, 3)
        .reshape(1, tok_rows, heads_local * HD)
    )
    cot_rows = cotangent[0].reshape(tok_rows, kv_local, group_size, HD)
    grad_terms = jnp.einsum(
        "gcts,tgcd->sgd", cross_weights, cot_rows, preferred_element_type=jnp.float32
    ).reshape(key_count, kv_local * HD)
    value_grad = lax.psum_scatter(
        grad_terms.astype(jnp.bfloat16), "seq", scatter_dimension=0, tiled=True
    )
    own_features = features[0]
    summed_samples = lax.psum_scatter(
        lax.dot_general(
            own_features, value_grad, (((0,), (0,)), ((), ())), preferred_element_type=jnp.float32
        ).astype(jnp.bfloat16),
        "dp",
        scatter_dimension=0,
        tiled=True,
    )
    weight_grad = lax.psum_scatter(summed_samples, "seq", scatter_dimension=0, tiled=True).astype(
        jnp.float32
    )
    return (merged, weight_grad)


def solution(mesh):
    in_specs = (
        P("dp", "seq", "tensor"),
        P("dp", "seq", "tensor"),
        P("dp", "seq", "tensor"),
        P("dp", "seq"),
        P("dp", "seq", "tensor"),
        P("dp", "seq", "tensor"),
        P("dp", "seq", "tensor"),
        P("dp", "seq", None),
        P(None, "tensor"),
        P("dp", None),
        P("dp", None),
    )
    out_specs = (P("dp", "seq", "tensor"), P(("dp", "seq"), "tensor"))
    return jax.shard_map(
        on_device, mesh=mesh, in_specs=in_specs, out_specs=out_specs, check_vma=False
    )
```

profile of v0, /device:TPU:0, one launch (start us, length us, event | category | flops | bytes accessed | tf_op | source)
XLA Modules:
  0.0 108.2 jit_solution(1521018898285160767)
XLA Ops:
  7.2 0.8 select_reduce_fusion
  8.1 1.4 %reshape_squeeze.10 = bf16[128,4,4,128]{3,2,1,0:T(4,128)(2,1)S(1)} reshape(bf16[1,128,2048]{2,1,0:T(8,128)(2,1)} %param.15) | data formatting | bytes 1048576 | tf_op jit(solution)/shard_map/reshape;squeeze | solution.py:107
  9.5 6.7 %all-gather = bf16[1,128,512]{2,1,0:T(8,128)(2,1)S(1)} all-gather(bf16[1,32,512]{2,1,0:T(8,128)(2,1)} %param.17), channel_id=2, replica_groups=mesh['dp'=4,'seq'=4,'tensor'=2] {'seq'}, dimensions={1}, use_global_device_ids=true | all-gather | bytes 163840 | tf_op jit(solution)/shard_map/all_gather | solution.py:92
  16.2 0.1 copy.56
  16.4 1.3 %copy.78 = bf16[1,128,2048]{1,2,0:T(8,128)(2,1)S(1)} copy(bf16[1,128,2048]{2,1,0:T(8,128)(2,1)} %param.16) | data formatting | bytes 1048576 | tf_op jit(solution)/shard_map/reshape;squeeze | solution.py:134
  17.7 0.8 select_reduce_fusion.1
  18.5 0.1 compare_and_fusion
  18.6 1.5 %fusion.39 = (f32[4,4,128]{2,1,0:T(4,128)S(1)}, f32[4,4,128,128]{2,3,1,0:T(8,128)}) fusion(bf16[128,4,128,1]{0,2,3,1:T(8,128)(2,1)S(1)} %bitcast.96, bf16[128,4,4,128]{3,2,1,0:T(4,128)(2,1)S(1)} %reshape_squeeze.10, pred[128,128]{0,1:T(8,128)(4,1)S(1)} %compare_and_fusion), kind=kOutput, calls=%fused_computation.53 | convolution fusion | flops 68419712 | bytes 1728512 | tf_op jit(solution)/shard_map/sub | solution.py:119
  20.1 1.6 %fusion.21 = bf16[4,128,128]{1,2,0:T(8,128)(2,1)S(1)} fusion(bf16[128,4,4,128]{0,3,2,1:T(8,128)(2,1)S(1)} %bitcast.94, f32[4,4,128,128]{2,3,1,0:T(8,128)} %get-tuple-element.48, f32[4,4,128]{2,1,0:T(4,128)S(1)} %get-tuple-element.47), kind=kOutput, calls=%fused_computation.22 | convolution fusion | flops 67698688 | bytes 1712128 | tf_op jit(solution)/shard_map/gcts,tgcd->sgd/dot_general | solution.py:135
  21.7 0.8 copy.79
  22.6 21.3 %reduce-scatter.10.cloned.1.call-done = bf16[32,512]{1,0:T(8,128)(2,1)} async-done(((bf16[128,512]{1,0:T(8,128)(2,1)}), bf16[32,512]{1,0:T(8,128)(2,1)}) %reduce-scatter.10.cloned.1.call-update) | async-done | bytes 32784
  43.9 1.3 %fusion.4 = bf16[1280,512]{0,1:T(8,128)(2,1)S(1)} fusion(bf16[32,512]{1,0:T(8,128)(2,1)} %reduce-scatter.10.cloned.1.call-done, bf16[1,32,1280]{2,1,0:T(8,128)(2,1)S(1)} %copy-done.2), kind=kOutput, calls=%fused_computation.7 | convolution fusion | flops 42598400 | bytes 1425408 | tf_op jit(solution)/shard_map/dot_general | solution.py:143
  45.2 1.5 %copy.81 = bf16[1280,512]{1,0:T(8,128)(2,1)} copy(bf16[1280,512]{0,1:T(8,128)(2,1)S(1)} %fusion.4) | data formatting | bytes 2621440
  46.8 0.1 copy.51
  47.0 0.4 reshape_squeeze.9
  47.3 6.5 %all_gather.17 = bf16[1,512,512]{2,1,0:T(8,128)(2,1)S(1)} all-gather(bf16[1,128,512]{2,1,0:T(8,128)(2,1)S(1)} %copy-done.3), channel_id=1, replica_groups=mesh['dp'=4,'seq'=4,'tensor'=2] {'seq'}, dimensions={1}, use_global_device_ids=true | all-gather | bytes 655360 | tf_op jit(solution)/shard_map/all_gather | solution.py:57
  53.8 0.2 copy.54
  54.1 5.1 %all_gather.15 = s32[1,512]{1,0:T(1,128)S(1)} all-gather(s32[1,128]{1,0:T(1,128)S(1)} %copy-done.5), channel_id=1, replica_groups=mesh['dp'=4,'seq'=4,'tensor'=2] {'seq'}, dimensions={1}, use_global_device_ids=true | all-gather | bytes 2560 | tf_op jit(solution)/shard_map/all_gather | solution.py:58
  59.1 7.3 %all_gather.16 = bf16[1,512,512]{1,2,0:T(8,128)(2,1)S(1)} all-gather(bf16[1,128,512]{1,2,0:T(8,128)(2,1)S(1)} %copy.51), channel_id=1, replica_groups=mesh['dp'=4,'seq'=4,'tensor'=2] {'seq'}, dimensions={1}, use_global_device_ids=true | all-gather | bytes 655360 | tf_op jit(solution)/shard_map/all_gather | solution.py:56
  66.4 0.1 fusion.25
  66.6 0.9 fusion.1
  67.5 1.0 fusion.2
  68.5 2.2 %fusion.17 = f32[128,4,4,128]{0,3,2,1:T(8,128)} fusion(bf16[512,4,128,1]{0,2,3,1:T(8,128)(2,1)S(1)} %bitcast.93, f32[4,512,128,4]{2,1,3,0:T(8,128)S(1)} %get-tuple-element.46, f32[4,4,128]{2,1,0:T(4,128)S(1)} %get-tuple-element.44, pred[128,512]{0,1:T(8,128)(4,1)S(1)} %fusion.25, f32[128,4,4]{0,2,1:T(4,128)S(1)} %get-tuple-element.32), kind=kOutput, calls=%fused_computation.19 | convolution fusion | flops 273940480 | bytes 5849088 | tf_op jit(solution)/shard_map/while/body/eval_jaxpr/gcts,sgd->gctd/dot_general | solution.py:30
  70.6 7.6 %reduce-scatter.12.cloned.1.call-done = bf16[320,512]{1,0:T(8,128)(2,1)} async-done(((bf16[1280,512]{1,0:T(8,128)(2,1)}), bf16[320,512]{1,0:T(8,128)(2,1)}) %reduce-scatter.12.cloned.1.call-update) | async-done | bytes 327696
  78.3 0.3 convolution_convert_fusion.1
  78.6 5.4 %all_gather.19 = bf16[128,512]{1,0:T(8,128)(2,1)S(1)} all-gather(bf16[32,512]{1,0:T(8,128)(2,1)S(1)} %convolution_convert_fusion.1), channel_id=1, replica_groups=mesh['dp'=4,'seq'=4,'tensor'=2] {'seq'}, dimensions={0}, use_global_device_ids=true | all-gather | bytes 163840 | tf_op jit(solution)/shard_map/all_gather | solution.py:93
  84.0 0.1 copy.77
  84.2 1.5 %fusion.20 = bf16[128,4,4,128]{0,3,2,1:T(8,128)(2,1)S(1)} fusion(bf16[128,4,128,1]{0,2,3,1:T(8,128)(2,1)S(1)} %bitcast.97, f32[128,4,4,128]{0,3,2,1:T(8,128)} %fusion.17, f32[128,4,4]{0,2,1:T(4,128)S(1)} %bitcast_add_fusion, f32[4,4,128,128]{2,3,1,0:T(8,128)S(1)} %copy-done.6, f32[4,4,128]{2,1,0:T(4,128)S(1)} %get-tuple-element.47), kind=kOutput, calls=%fused_computation.20 | convolution fusion | flops 68419584 | bytes 2768896 | tf_op jit(solution)/shard_map/gcts,sgd->gctd/dot_general | solution.py:122
  85.7 1.0 copy.63
  86.7 13.2 %reduce-scatter.14.cloned.1.call-done = bf16[80,512]{1,0:T(8,128)(2,1)} async-done(((bf16[320,512]{1,0:T(8,128)(2,1)}), bf16[80,512]{1,0:T(8,128)(2,1)}) %reduce-scatter.14.cloned.1.call-update) | async-done | bytes 81936
  99.9 1.0 copy.84
  100.9 0.8 copy.64
  (25 shorter events, 0.3 us)
Async XLA Ops:
  7.2 71.1 %copy-start = (bf16[1280,512]{1,0:T(8,128)(2,1)S(1)}, bf16[1280,512]{1,0:T(8,128)(2,1)}, u32[]{:S(2)}) copy-start(bf16[1280,512]{1,0:T(8,128)(2,1)} %param.19) | copy-start | bytes 3932164
  7.2 36.8 %reduce-scatter.10.cloned.1.call-start = ((), (), s32[]{:S(2)}) async-start(), calls=%async_computation.3 | async-start | bytes 163840
  16.4 27.6 %copy-start.2 = (bf16[1,32,1280]{2,1,0:T(8,128)(2,1)S(1)}, bf16[1,32,1280]{2,1,0:T(8,128)(2,1)}, u32[]{:S(2)}) copy-start(bf16[1,32,1280]{2,1,0:T(8,128)(2,1)} %param.18) | copy-start | bytes 245764
  20.1 26.7 %copy-start.4 = (bf16[1,128,512]{2,1,0:T(8,128)(2,1)S(1)}, bf16[1,128,512]{2,1,0:T(8,128)(2,1)}, u32[]{:S(2)}) copy-start(bf16[1,128,512]{2,1,0:T(8,128)(2,1)} %param.12) | copy-start | bytes 393220
  20.1 26.8 %copy-start.1 = (bf16[1,128,2048]{2,1,0:T(8,128)(2,1)S(1)}, bf16[1,128,2048]{2,1,0:T(8,128)(2,1)}, u32[]{:S(2)}) copy-start(bf16[1,128,2048]{2,1,0:T(8,128)(2,1)} %param.11) | copy-start | bytes 1572868
  21.7 25.6 %copy-start.3 = (bf16[1,128,512]{2,1,0:T(8,128)(2,1)S(1)}, bf16[1,128,512]{2,1,0:T(8,128)(2,1)}, u32[]{:S(2)}) copy-start(bf16[1,128,512]{2,1,0:T(8,128)(2,1)} %param.13) | copy-start | bytes 393220
  22.5 31.5 %copy-start.5 = (s32[1,128]{1,0:T(1,128)S(1)}, s32[1,128]{1,0:T(1,128)}, u32[]{:S(2)}) copy-start(s32[1,128]{1,0:T(1,128)} %param.14) | copy-start | bytes 1540
  22.6 55.7 %reduce-scatter.12.cloned.1.call-start = ((), (), s32[]{:S(2)}) async-start(), calls=%async_computation.4 | async-start | bytes 1638400
  46.8 53.2 %reduce-scatter.14.cloned.1.call-start = ((), (), s32[]{:S(2)}) async-start(), calls=%async_computation.5 | async-start | bytes 409600
  68.5 15.7 %copy-start.6 = (f32[4,4,128,128]{2,3,1,0:T(8,128)S(1)}, f32[4,4,128,128]{2,3,1,0:T(8,128)}, u32[]{:S(2)}) copy-start(f32[4,4,128,128]{2,3,1,0:T(8,128)} %get-tuple-element.48) | copy-start | bytes 3145732
Sparse Core Ops, SparseCore 0:
  22.7 21.2 reduce-scatter.9
  46.9 31.3 reduce-scatter.11
  80.8 19.1 reduce-scatter.13
where the time goes:
time: 109 us; the launch traced here: 108 us
  waiting for transfers between devices  42.2 us (39%)
  blocking collectives  31 us (28%)
  between operations  14 us (13%)
  matrix products  9.32 us (9%)
  local copies, waits for them, and re-layouts  8.77 us (8%)
  other arithmetic  2.87 us (3%)
    unnamed x6, waiting for transfers between devices  42.2 us
    all_gather x1, blocking collectives, on_device(): piece_keys = lax.all_gather(k_self, 'seq', axis=1, tiled=True)  7.28 us
    all_gather x1, blocking collectives, on_device(): lax.all_gather(img_keys[0], 'seq', axis=0, tiled=True)  6.75 us
    all_gather x1, blocking collectives, on_device(): piece_values = lax.all_gather(v_self, 'seq', axis=1, tiled=True)  6.5 us
    all_gather x1, blocking collectives, on_device(): lax.all_gather(values_own, 'seq', axis=0, tiled=True)  5.42 us
    unnamed x20, local copies, waits for them, and re-layouts  5.21 us
    all_gather x1, blocking collectives, on_device(): piece_docs = lax.all_gather(docs, 'seq', axis=1, tiled=True)  5.06 us
  transfers between devices with their start and end apart: 3, of which 3 were waited for; matrix products, arithmetic and copies ran while one was open for 7% of the time, Pallas kernels for 0%

commit v1 on v0

--- a/solution.py
+++ b/solution.py
@@ -53,7 +53,19 @@
         jnp.zeros((kv_local, group_size, tok_rows), jnp.float32),
         jnp.zeros((kv_local, group_size, tok_rows, HD), jnp.float32),
     )
-    piece_keys = lax.all_gather(k_self, "seq", axis=1, tiled=True)
+
+    def refer_series_all_for(sheet, named_axis):
+        nodes = lax.axis_size(named_axis)
+        h_now = [(c - 1, c) for c in range(1, nodes)] + [(nodes - 1, 0)]
+        val = sheet
+        entries = [val]
+        for _ in range(nodes - 1):
+            val = lax.ppermute(val, axis_name=named_axis, perm=h_now)
+            entries += [val]
+        base_arr = jnp.concatenate([*reversed(entries)], axis=1)
+        return jnp.roll(base_arr, (lax.axis_index(named_axis) + 1) * val.shape[1], axis=1)
+
+    piece_keys = refer_series_all_for(k_self, "seq")
     piece_values = lax.all_gather(v_self, "seq", axis=1, tiled=True)
     piece_docs = lax.all_gather(docs, "seq", axis=1, tiled=True)
     key_count = piece_keys.shape[1]

time: 109 us -> 109 us (level)
  blocking collectives: 31 us -> 24.3 us
  other arithmetic: 2.87 us -> 5.16 us
  local copies, waits for them, and re-layouts: 8.77 us -> 11 us
    all_gather x1 -> x0, blocking collectives: 7.28 us -> none  [on_device(): piece_keys = lax.all_gather(k_self, 'seq', axis=1, tiled=True)]
    ppermute x0 -> x3, waiting for transfers between devices: none -> 3.92 us  [refer_series_all_for(): val = lax.ppermute(val, axis_name=named_axis, perm=h_now)]
    unnamed x6, waiting for transfers between devices: 42.2 us -> 39.3 us
    reduce_sum x1, other arithmetic: 1.01 us -> 3.27 us  [absorb_block(): denominator = factor * denominator + jnp.sum(weights, axis=-1)]
    unnamed x20 -> x27, local copies, waits for them, and re-layouts: 5.21 us -> 7.36 us
  transfers between devices with their start and end apart: 3 -> 6, of which waited for: 3 -> 4; matrix products, arithmetic and copies ran while one was open for 7% -> 12% of each run, Pallas kernels for 0% -> 0%
where the time goes in v1:
time: 109 us; the launch traced here: 108 us
  waiting for transfers between devices  43.2 us (40%)
  blocking collectives  24.3 us (22%)
  between operations  14 us (13%)
  local copies, waits for them, and re-layouts  11 us (10%)
  matrix products  9.31 us (9%)
  other arithmetic  5.16 us (5%)
  starting transfers between devices  1.21 us (1%)
    unnamed x6, waiting for transfers between devices  39.3 us
    unnamed x27, local copies, waits for them, and re-layouts  7.36 us
    all_gather x1, blocking collectives, on_device(): lax.all_gather(img_keys[0], 'seq', axis=0, tiled=True)  6.75 us
    all_gather x1, blocking collectives, on_device(): piece_values = lax.all_gather(v_self, 'seq', axis=1, tiled=True)  6.71 us
    all_gather x1, blocking collectives, on_device(): lax.all_gather(values_own, 'seq', axis=0, tiled=True)  5.8 us
    all_gather x1, blocking collectives, on_device(): piece_docs = lax.all_gather(docs, 'seq', axis=1, tiled=True)  5.06 us
    ppermute x3, waiting for transfers between devices, refer_series_all_for(): val = lax.ppermute(val, axis_name=named_axis, perm=h_now)  3.92 us
    reduce_sum x1, other arithmetic, absorb_block(): denominator = factor * denominator + jnp.sum(weights, axis=-1)  3.27 us
  transfers between devices with their start and end apart: 6, of which 4 were waited for; matrix products, arithmetic and copies ran while one was open for 12% of the time, Pallas kernels for 0%

profile of v1, /device:TPU:0, one launch (start us, length us, event | category | flops | bytes accessed | tf_op | source)
XLA Modules:
  0.0 108.2 jit_solution(17699315524621244304)
XLA Ops:
  7.2 0.8 select_reduce_fusion
  8.1 1.4 %reshape_squeeze.10 = bf16[128,4,4,128]{3,2,1,0:T(4,128)(2,1)S(1)} reshape(bf16[1,128,2048]{2,1,0:T(8,128)(2,1)} %param.15) | data formatting | bytes 1048576 | tf_op jit(solution)/shard_map/reshape;squeeze | solution.py:119
  9.5 6.7 %all-gather = bf16[1,128,512]{2,1,0:T(8,128)(2,1)S(1)} all-gather(bf16[1,32,512]{2,1,0:T(8,128)(2,1)} %param.17), channel_id=2, replica_groups=mesh['dp'=4,'seq'=4,'tensor'=2] {'seq'}, dimensions={1}, use_global_device_ids=true | all-gather | bytes 163840 | tf_op jit(solution)/shard_map/all_gather | solution.py:104
  16.4 1.3 %copy.84 = bf16[1,128,2048]{1,2,0:T(8,128)(2,1)S(1)} copy(bf16[1,128,2048]{2,1,0:T(8,128)(2,1)} %param.16) | data formatting | bytes 1048576 | tf_op jit(solution)/shard_map/reshape;squeeze | solution.py:146
  17.7 0.8 select_reduce_fusion.1
  18.6 1.6 %fusion.39 = (f32[4,4,128]{2,1,0:T(4,128)S(1)}, f32[4,4,128,128]{2,3,1,0:T(8,128)}) fusion(bf16[128,4,128,1]{0,2,3,1:T(8,128)(2,1)S(1)} %bitcast.97, bf16[128,4,4,128]{3,2,1,0:T(4,128)(2,1)S(1)} %reshape_squeeze.10, pred[128,128]{0,1:T(8,128)(4,1)S(1)} %compare_and_fusion), kind=kOutput, calls=%fused_computation.62 | convolution fusion | flops 68419712 | bytes 1728512 | tf_op jit(solution)/shard_map/sub | solution.py:131
  20.2 1.5 %fusion.21 = bf16[4,128,128]{1,2,0:T(8,128)(2,1)S(1)} fusion(bf16[128,4,4,128]{0,3,2,1:T(8,128)(2,1)S(1)} %bitcast.94, f32[4,4,128,128]{2,3,1,0:T(8,128)} %get-tuple-element.48, f32[4,4,128]{2,1,0:T(4,128)S(1)} %get-tuple-element.47), kind=kOutput, calls=%fused_computation.22 | convolution fusion | flops 67698688 | bytes 1712128 | tf_op jit(solution)/shard_map/gcts,tgcd->sgd/dot_general | solution.py:147
  21.7 0.8 copy.85
  22.7 0.4 collective-permute-start
  23.1 0.3 convolution_convert_fusion.1
  23.4 20.5 %reduce-scatter.10.cloned.1.call-done = bf16[32,512]{1,0:T(8,128)(2,1)} async-done(((bf16[128,512]{1,0:T(8,128)(2,1)}), bf16[32,512]{1,0:T(8,128)(2,1)}) %reduce-scatter.10.cloned.1.call-update) | async-done | bytes 32784
  43.9 1.3 %fusion.4 = bf16[1280,512]{0,1:T(8,128)(2,1)S(1)} fusion(bf16[32,512]{1,0:T(8,128)(2,1)} %reduce-scatter.10.cloned.1.call-done, bf16[1,32,1280]{2,1,0:T(8,128)(2,1)S(1)} %copy-done.3), kind=kOutput, calls=%fused_computation.7 | convolution fusion | flops 42598400 | bytes 1425408 | tf_op jit(solution)/shard_map/dot_general | solution.py:155
  45.2 1.5 %copy.87 = bf16[1280,512]{1,0:T(8,128)(2,1)} copy(bf16[1280,512]{0,1:T(8,128)(2,1)S(1)} %fusion.4) | data formatting | bytes 2621440
  46.8 6.7 %all_gather.13 = bf16[1,512,512]{2,1,0:T(8,128)(2,1)S(1)} all-gather(bf16[1,128,512]{2,1,0:T(8,128)(2,1)} %param.13), channel_id=1, replica_groups=mesh['dp'=4,'seq'=4,'tensor'=2] {'seq'}, dimensions={1}, use_global_device_ids=true | all-gather | bytes 655360 | tf_op jit(solution)/shard_map/all_gather | solution.py:69
  53.5 0.3 collective-permute-start.1
  53.8 5.8 %all_gather.15 = bf16[128,512]{1,0:T(8,128)(2,1)S(1)} all-gather(bf16[32,512]{1,0:T(8,128)(2,1)S(1)} %convolution_convert_fusion.1), channel_id=1, replica_groups=mesh['dp'=4,'seq'=4,'tensor'=2] {'seq'}, dimensions={0}, use_global_device_ids=true | all-gather | bytes 163840 | tf_op jit(solution)/shard_map/all_gather | solution.py:105
  59.6 0.4 reshape_squeeze.9
  60.0 0.2 copy.60
  60.4 5.1 %all_gather.12 = s32[1,512]{1,0:T(1,128)S(1)} all-gather(s32[1,128]{1,0:T(1,128)S(1)} %copy-done.5), channel_id=1, replica_groups=mesh['dp'=4,'seq'=4,'tensor'=2] {'seq'}, dimensions={1}, use_global_device_ids=true | all-gather | bytes 2560 | tf_op jit(solution)/shard_map/all_gather | solution.py:70
  65.4 0.3 collective-permute-start.2
  65.8 0.1 fusion.25
  65.9 3.9 %collective-permute-done.2 = bf16[1,128,512]{1,2,0:T(8,128)(2,1)S(1)} collective-permute-done((bf16[1,128,512]{1,2,0:T(8,128)(2,1)S(1)}, bf16[1,128,512]{1,2,0:T(8,128)(2,1)S(1)}, u32[]{:S(2)}, u32[]{:S(2)}) %collective-permute-start.2) | collective-permute-done | bytes 131104 | tf_op jit(solution)/shard_map/ppermute | solution.py:63
  70.3 0.9 fusion.1
  71.2 1.9 %copy-done.1 = f32[4,512,128,4]{2,1,3,0:T(8,128)} copy-done((f32[4,512,128,4]{2,1,3,0:T(8,128)}, f32[4,512,128,4]{2,1,3,0:T(8,128)S(1)}, u32[]{:S(2)}) %copy-start.1) | copy-done | bytes 4194328
  73.1 2.2 %fusion.17 = f32[128,4,4,128]{0,3,2,1:T(8,128)} fusion(bf16[512,4,128,1]{0,2,3,1:T(8,128)(2,1)S(1)} %bitcast.93, f32[4,512,128,4]{2,1,3,0:T(8,128)S(1)} %get-tuple-element.46, f32[4,4,128]{2,1,0:T(4,128)S(1)} %get-tuple-element.44, pred[128,512]{0,1:T(8,128)(4,1)S(1)} %fusion.25, f32[128,4,4]{0,2,1:T(4,128)S(1)} %get-tuple-element.32), kind=kOutput, calls=%fused_computation.19 | convolution fusion | flops 273940480 | bytes 5849088 | tf_op jit(solution)/shard_map/while/body/eval_jaxpr/gcts,sgd->gctd/dot_general | solution.py:30
  75.3 3.0 %reduce-scatter.12.cloned.1.call-done = bf16[320,512]{1,0:T(8,128)(2,1)} async-done(((bf16[1280,512]{1,0:T(8,128)(2,1)}), bf16[320,512]{1,0:T(8,128)(2,1)}) %reduce-scatter.12.cloned.1.call-update) | async-done | bytes 327696
  78.3 3.3 %fusion.2 = f32[4,4,128]{2,1,0:T(4,128)S(1)} fusion(f32[4,512,128,4]{2,1,3,0:T(8,128)} %copy-done.1, f32[4,4,128]{2,1,0:T(4,128)S(1)} %get-tuple-element.44, pred[128,512]{0,1:T(8,128)(4,1)S(1)} %fusion.25), kind=kLoop, calls=%fused_computation.5 | loop fusion | flops 5240832 | bytes 4276224 | tf_op jit(solution)/shard_map/while/body/eval_jaxpr/reduce_sum | solution.py:29
  81.6 1.5 %fusion.20 = bf16[128,4,4,128]{0,3,2,1:T(8,128)(2,1)S(1)} fusion(bf16[128,4,128,1]{0,2,3,1:T(8,128)(2,1)S(1)} %bitcast.96, f32[128,4,4,128]{0,3,2,1:T(8,128)S(1)} %copy-done.6, f32[128,4,4]{0,2,1:T(4,128)S(1)} %bitcast_add_fusion, f32[4,4,128,128]{2,3,1,0:T(8,128)} %get-tuple-element.48, f32[4,4,128]{2,1,0:T(4,128)S(1)} %get-tuple-element.47), kind=kOutput, calls=%fused_computation.20 | convolution fusion | flops 68419584 | bytes 2768896 | tf_op jit(solution)/shard_map/gcts,sgd->gctd/dot_general | solution.py:134
  83.1 1.0 copy.69
  84.1 15.8 %reduce-scatter.14.cloned.1.call-done = bf16[80,512]{1,0:T(8,128)(2,1)} async-done(((bf16[320,512]{1,0:T(8,128)(2,1)}), bf16[80,512]{1,0:T(8,128)(2,1)}) %reduce-scatter.14.cloned.1.call-update) | async-done | bytes 81936
  99.9 1.0 copy.90
  100.9 0.8 copy.70
  (39 shorter events, 1.0 us)
Async XLA Ops:
  7.2 16.0 %copy-start = (bf16[1280,512]{1,0:T(8,128)(2,1)S(1)}, bf16[1280,512]{1,0:T(8,128)(2,1)}, u32[]{:S(2)}) copy-start(bf16[1280,512]{1,0:T(8,128)(2,1)} %param.19) | copy-start | bytes 3932164
  7.2 36.8 %reduce-scatter.10.cloned.1.call-start = ((), (), s32[]{:S(2)}) async-start(), calls=%async_computation.3 | async-start | bytes 163840
  16.4 6.2 %copy-start.4 = (bf16[1,128,512]{2,1,0:T(8,128)(2,1)S(1)}, bf16[1,128,512]{2,1,0:T(8,128)(2,1)}, u32[]{:S(2)}) copy-start(bf16[1,128,512]{2,1,0:T(8,128)(2,1)} %param.12) | copy-start | bytes 393220
  17.7 5.4 %copy-start.3 = (bf16[1,32,1280]{2,1,0:T(8,128)(2,1)S(1)}, bf16[1,32,1280]{2,1,0:T(8,128)(2,1)}, u32[]{:S(2)}) copy-start(bf16[1,32,1280]{2,1,0:T(8,128)(2,1)} %param.18) | copy-start | bytes 245764
  21.7 37.9 %copy-start.2 = (bf16[1,128,2048]{2,1,0:T(8,128)(2,1)S(1)}, bf16[1,128,2048]{2,1,0:T(8,128)(2,1)}, u32[]{:S(2)}) copy-start(bf16[1,128,2048]{2,1,0:T(8,128)(2,1)} %param.11) | copy-start | bytes 1572868
  22.5 55.7 %reduce-scatter.12.cloned.1.call-start = ((), (), s32[]{:S(2)}) async-start(), calls=%async_computation.4 | async-start | bytes 1638400
  22.7 30.8 %collective-permute-start = (bf16[1,128,512]{1,2,0:T(8,128)(2,1)S(1)}, bf16[1,128,512]{1,2,0:T(8,128)(2,1)S(1)}, u32[]{:S(2)}, u32[]{:S(2)}) collective-permute-start(bf16[1,128,512]{1,2,0:T(8,128)(2,1)S(1)} %copy.55), channel_id=1, source_target_pairs={{0,2},{2,4},{4,6},{6,0},{1,3},{3,5},{5,7},{7,1},{8,10},{10,12},{12... | collective-permute-start | bytes 393224 | tf_op jit(solution)/shard_map/ppermute | solution.py:63
  23.4 36.9 %copy-start.5 = (s32[1,128]{1,0:T(1,128)S(1)}, s32[1,128]{1,0:T(1,128)}, u32[]{:S(2)}) copy-start(s32[1,128]{1,0:T(1,128)} %param.14) | copy-start | bytes 1540
  46.7 53.2 %reduce-scatter.14.cloned.1.call-start = ((), (), s32[]{:S(2)}) async-start(), calls=%async_computation.5 | async-start | bytes 409600
  53.5 11.9 %collective-permute-start.1 = (bf16[1,128,512]{1,2,0:T(8,128)(2,1)S(1)}, bf16[1,128,512]{1,2,0:T(8,128)(2,1)S(1)}, u32[]{:S(2)}, u32[]{:S(2)}) collective-permute-start(bf16[1,128,512]{1,2,0:T(8,128)(2,1)S(1)} %collective-permute-done), channel_id=1, source_target_pairs={{0,2},{2,4},{4,6},{6,0},{1,3},{3,5},{5,7},{7,1},{8,10},{10,12},{12... | collective-permute-start | bytes 393224 | tf_op jit(solution)/shard_map/ppermute | solution.py:63
  65.4 4.4 %collective-permute-start.2 = (bf16[1,128,512]{1,2,0:T(8,128)(2,1)S(1)}, bf16[1,128,512]{1,2,0:T(8,128)(2,1)S(1)}, u32[]{:S(2)}, u32[]{:S(2)}) collective-permute-start(bf16[1,128,512]{1,2,0:T(8,128)(2,1)S(1)} %collective-permute-done.1), channel_id=1, source_target_pairs={{0,2},{2,4},{4,6},{6,0},{1,3},{3,5},{5,7},{7,1},{8,10},{10,12},{12... | collective-permute-start | bytes 393224 | tf_op jit(solution)/shard_map/ppermute | solution.py:63
  71.2 1.9 %copy-start.1 = (f32[4,512,128,4]{2,1,3,0:T(8,128)}, f32[4,512,128,4]{2,1,3,0:T(8,128)S(1)}, u32[]{:S(2)}) copy-start(f32[4,512,128,4]{2,1,3,0:T(8,128)S(1)} %get-tuple-element.46) | copy-start | bytes 12582916
  78.3 3.3 %copy-start.6 = (f32[128,4,4,128]{0,3,2,1:T(8,128)S(1)}, f32[128,4,4,128]{0,3,2,1:T(8,128)}, u32[]{:S(2)}) copy-start(f32[128,4,4,128]{0,3,2,1:T(8,128)} %fusion.17) | copy-start | bytes 3145732
Sparse Core Ops, SparseCore 0:
  22.7 21.2 reduce-scatter.9
  46.9 31.3 reduce-scatter.11
  80.7 19.1 reduce-scatter.13
